TPU v7x, 32 devices: a whole 2x2x4 slice. The times are simulated.
32 devices in a mesh: patch: 16 (over z, y, core), chan: 2 (over x).
Axes of the slice: x: 2, y: 2, z: 4, core: 2. Of those that a mesh axis runs over, the one named last changes fastest.
Arguments:
- fields: bfloat16 [16, 128, 1024], P('patch', 'chan'), may hold values from -6 to 6
- w_one: bfloat16 [9, 512, 128], P(None, 'chan'), may hold values from -0.1875 to 0.1875
- bias_one: float32 [512], P('chan'), may hold values from -3 to 3
- w_two: bfloat16 [9, 128, 512], P(None, None, 'chan'), may hold values from -0.09375 to 0.09375
- neighbour: int32 [16, 4], replicated, may hold values from 0 to 15, as said below
- seam_code: int32 [16, 4], replicated, may hold values from 0 to 7, as said below
- band_order: int32 [16], replicated, may hold values from 0 to 15, each once
- target: bfloat16 [16, 128, 1024], P('patch', 'chan'), may hold values from -6 to 6
- lat_weight: bfloat16 [16, 1024], P('patch'), may hold values from 0.099609375 to 1
Outputs:
- loss_value: float32 [], replicated
- grad_one: float32 [9, 512, 128], P(None, 'chan')
- grad_two: float32 [9, 128, 512], P(None, None, 'chan')
- grad_bias: float32 [512], P('chan')
Inputs may be any that keep to these rules, and one draw needn't show every extreme that they name: The sides of all patches are paired: side s of patch p borders side t = seam_code[p, s] mod 4 of patch q = neighbour[p, s], and then neighbour[q, t] = p, seam_code[q, t] mod 4 = s, and both codes agree on being 4 or more; so every edge is read by exactly one side of one other patch, and the four sides of a patch face four different patches. `seam_code`: code mod 4 names the neighbour's edge that forms the seam; codes 4 and above run that edge reversed, alike on both sides of a seam. `band_order`: each patch fills exactly one slot of every band.
All inputs are finite; a program needn't handle non-finite values.
Results may differ from a plain program's by a relative error of at most 0.0021.
Values may be sent and summed in bfloat16 or wider, within the bound.
A program may use at most 64 MiB of HBM per device.

v0:
```python
import math
import jax
import jax.numpy as jnp
from jax import lax
from jax.sharding import PartitionSpec as P

C = 128
P_SIZE = 32


def edges_of(field):
    return jnp.stack(
        [field[..., 0, :], field[..., -1, :], field[..., :, 0], field[..., :, -1]], axis=-3
    )


def with_frame(field, strips):
    padded = jnp.pad(field, ((0, 0), (1, 1), (1, 1)))
    padded = padded.at[:, 0, 1:-1].set(strips[0])
    padded = padded.at[:, -1, 1:-1].set(strips[1])
    padded = padded.at[:, 1:-1, 0].set(strips[2])
    padded = padded.at[:, 1:-1, -1].set(strips[3])
    return padded


def tap_list(padded):
    length = padded.shape[-1] - 2
    span = length + 2
    flat = jnp.pad(padded.reshape(padded.shape[0], span * span), ((0, 0), (0, 2)))
    return [
        flat[:, row_off * span + col_off : row_off * span + col_off + length * span]
        for row_off in range(3)
        for col_off in range(3)
    ]


def narrow(wide, length):
    return wide.reshape(wide.shape[0], length, length + 2)[:, :, :length].reshape(
        wide.shape[0], length * length
    )


def widen(values, length):
    shaped = values.reshape(values.shape[0], length, length)
    return jnp.pad(shaped, ((0, 0), (0, 0), (0, 2))).reshape(values.shape[0], length * (length + 2))


def apply_taps(weight, taps):
    summed = jnp.zeros((weight.shape[1], taps[0].shape[1]), jnp.float32)
    for tap_index in range(9):
        summed = summed + jnp.dot(
            weight[tap_index], taps[tap_index], preferred_element_type=jnp.float32
        )
    return summed


def smooth_gate(values):
    return jax.nn.gelu(values, approximate=True)


def oriented(strips, codes):
    return jnp.where((codes >= 4)[:, None, None], strips[..., ::-1], strips)


def on_device(fields, w_one, bias_one, w_two, neighbour, seam_code, band_order, target, lat_weight):
    length = P_SIZE
    span = P_SIZE + 2
    cell_count = P_SIZE * P_SIZE
    patch_count = lax.axis_size("patch")
    part_len = cell_count // patch_count
    own_index = lax.axis_index("patch")
    own_nbr = lax.dynamic_slice_in_dim(neighbour, own_index, 1, 0)[0]
    own_code = lax.dynamic_slice_in_dim(seam_code, own_index, 1, 0)[0]
    sides = jnp.arange(4, dtype=jnp.int32)

    def pick_edges(shard_rows):
        row_ids = jnp.arange(shard_rows.shape[0], dtype=jnp.int32)
        chosen = (own_nbr[:, None, None] == row_ids[None, :, None]) & (
            (own_code % 4)[:, None, None] == sides[None, None, :]
        )
        return jnp.einsum(
            "srt,rtcq->scq",
            chosen.astype(shard_rows.dtype),
            shard_rows,
            preferred_element_type=jnp.float32,
        )

    local = fields[0]
    local_ch = local.shape[0]
    whole = lax.all_gather(local, "chan", axis=0, tiled=True)
    grid = whole.reshape(whole.shape[0], length, length)
    seams = pick_edges(lax.all_gather(edges_of(grid)[None], "patch", axis=0, tiled=True))
    x_pad = with_frame(grid, oriented(seams, own_code).astype(jnp.bfloat16))
    x_taps = tap_list(x_pad)
    preact = narrow(apply_taps(w_one, x_taps), length) + bias_one[:, None]
    hidden = smooth_gate(preact).astype(jnp.bfloat16)
    inner_ch = hidden.shape[0]
    hidden_grid = hidden.reshape(inner_ch, length, length)
    hidden_seams = pick_edges(
        lax.all_gather(edges_of(hidden_grid)[None], "patch", axis=0, tiled=True)
    )
    hidden_strips = oriented(hidden_seams, own_code).astype(jnp.bfloat16)
    h_pad = with_frame(hidden_grid, hidden_strips)
    h_taps = tap_list(h_pad)
    mixed = lax.psum_scatter(
        narrow(apply_taps(w_two, h_taps), length), "chan", scatter_dimension=0, tiled=True
    )
    outputs = local.astype(jnp.float32) + mixed
    inv_root = 1.0 / math.sqrt(patch_count * cell_count)
    inverse = (
        jnp.zeros((patch_count,), jnp.int32)
        .at[band_order]
        .set(jnp.arange(patch_count, dtype=jnp.int32))
    )
    arrived = lax.all_to_all(
        outputs.reshape(local_ch, patch_count, part_len),
        "patch",
        split_axis=1,
        concat_axis=1,
        tiled=True,
    )
    in_band = arrived[:, band_order, :].reshape(local_ch, cell_count)
    misfit = in_band - target[0].astype(jnp.float32)
    lat_w = lat_weight[0].astype(jnp.float32)[None, :]
    partial_loss = jnp.sum(lat_w * misfit * misfit)
    band_grad = (
        (lat_w * misfit * inv_root).astype(jnp.bfloat16).reshape(local_ch, patch_count, part_len)
    )
    returned = lax.all_to_all(
        band_grad[:, inverse, :], "patch", split_axis=1, concat_axis=1, tiled=True
    )
    grad_out = returned.reshape(local_ch, cell_count)
    loss_value = lax.psum(partial_loss, ("patch", "chan")) / (patch_count * cell_count * C)
    grad_full = lax.all_gather(grad_out, "chan", axis=0, tiled=True)
    grad_wide = widen(grad_full, length)
    flat_len = span * span + 2
    wide_len = length * span
    frame_flat = jnp.zeros((inner_ch, flat_len), jnp.float32)
    tap_index = 0
    for row_off in range(3):
        for col_off in range(3):
            block = lax.dot_general(
                w_two[tap_index],
                grad_wide,
                (((0,), (0,)), ((), ())),
                preferred_element_type=jnp.float32,
            )
            offset = row_off * span + col_off
            frame_flat = frame_flat + jnp.pad(
                block, ((0, 0), (offset, flat_len - offset - wide_len))
            )
            tap_index = tap_index + 1
    grad_frame = frame_flat[:, : span * span].reshape(inner_ch, span, span)
    interior = grad_frame[:, 1:-1, 1:-1]
    frames = jnp.stack(
        [
            grad_frame[:, 0, 1:-1],
            grad_frame[:, -1, 1:-1],
            grad_frame[:, 1:-1, 0],
            grad_frame[:, 1:-1, -1],
        ]
    )
    shard_rows = lax.all_gather(frames[None], "patch", axis=0, tiled=True)
    matched = (neighbour == own_index)[:, :, None] & (
        (seam_code % 4)[:, :, None] == sides[None, None, :]
    )
    keep_same = (matched & (seam_code < 4)[:, :, None]).astype(jnp.float32)
    keep_turned = (matched & (seam_code >= 4)[:, :, None]).astype(jnp.float32)
    running = jnp.einsum("rst,rsep->tep", keep_same, shard_rows, precision=lax.Precision.HIGHEST)
    edge_back = running + jnp.einsum(
        "rst,rsep->tep", keep_turned, shard_rows[..., ::-1], precision=lax.Precision.HIGHEST
    )
    grad_h = interior.at[:, 0, :].add(edge_back[0])
    grad_h = grad_h.at[:, -1, :].add(edge_back[1])
    grad_h = grad_h.at[:, :, 0].add(edge_back[2])
    grad_h = grad_h.at[:, :, -1].add(edge_back[3])
    grad_h = grad_h.reshape(inner_ch, cell_count)
    grad_pre = jax.vjp(smooth_gate, preact)[1](grad_h)[0]
    bias_local = jnp.sum(grad_pre, axis=1)
    pre_wide = widen(grad_pre.astype(jnp.bfloat16), length)
    one_local = jnp.stack(
        [
            lax.dot_general(
                pre_wide, x_taps[idx], (((1,), (1,)), ((), ())), preferred_element_type=jnp.float32
            )
            for idx in range(9)
        ]
    )
    two_local = jnp.stack(
        [
            lax.dot_general(
                grad_wide, h_taps[idx], (((1,), (1,)), ((), ())), preferred_element_type=jnp.float32
            )
            for idx in range(9)
        ]
    )
    grad_one, grad_two, grad_bias = lax.psum((one_local, two_local, bias_local), "patch")
    return (loss_value, grad_one, grad_two, grad_bias)


def solution(mesh):
    placed = (
        P("patch", "chan", None),
        P(None, "chan", None),
        P("chan"),
        P(None, None, "chan"),
        P(),
        P(),
        P(),
        P("patch", "chan", None),
        P("patch", None),
    )
    return jax.shard_map(
        on_device,
        mesh=mesh,
        in_specs=placed,
        out_specs=(P(), P(None, "chan", None), P(None, None, "chan"), P("chan")),
        check_vma=False,
    )
```

profile of v0, /device:TPU:0, one launch (start us, length us, event | category | flops | bytes accessed | tf_op | source)
XLA Modules:
  0.0 331.3 jit_solution(5937897365871116879)
XLA Ops:
  7.2 7.4 %all-gather = bf16[1,128,1024]{2,1,0:T(8,128)(2,1)S(1)} all-gather(bf16[1,64,1024]{2,1,0:T(8,128)(2,1)} %param.33), channel_id=2, replica_groups=mesh['patch'=16,'chan'=2] {'chan'}, dimensions={1}, use_global_device_ids=true | all-gather | bytes 393216 | tf_op jit(solution)/shard_map/all_gather | solution.py:90
  15.8 23.5 %all-gather.1 = bf16[64,128,32]{1,2,0:T(8,128)(2,1)S(1)} all-gather(bf16[4,128,32]{1,2,0:T(8,128)(2,1)S(1)} %pad_maximum_fusion.2), channel_id=3, replica_groups=mesh['patch'=16,'chan'=2] {'patch'}, dimensions={0}, use_global_device_ids=true | all-gather | bytes 557056 | tf_op jit(solution)/shard_map/all_gather | solution.py:92
  40.6 1.5 scatter.34
  47.8 35.0 %all-gather.7.cloned.1.call-done = bf16[64,256,32]{1,2,0:T(8,128)(2,1)} async-done(((bf16[4,256,32]{1,2,0:T(8,128)(2,1)}), bf16[64,256,32]{1,2,0:T(8,128)(2,1)}) %all-gather.7.cloned.1.call-update) | async-done | bytes 1048592 | tf_op jit(solution)/shard_map/all_gather | solution.py:100
  82.7 2.0 convolution_bitcast_fusion.27
  85.0 1.5 scatter.40
  90.3 1.0 copy.93
  91.5 13.4 %reduce-scatter.4.cloned.1.call-done = f32[64,1024]{1,0:T(8,128)} async-done(((f32[128,1024]{1,0:T(8,128)}), f32[64,1024]{1,0:T(8,128)}) %reduce-scatter.4.cloned.1.call-update) | async-done | bytes 262160
  104.9 1.1 copy.94
  106.3 1.0 reshape.635
  107.4 5.6 %all-to-all-start = ((f32[16,1,4096]{2,1,0:T(1,128)}), f32[16,1,4096]{2,1,0:T(1,128)S(1)}, u32[]{:S(2)}, u32[]{:S(2)}) async-start(f32[16,1,4096]{2,1,0:T(1,128)} %reshape.635), calls=%async_computation | async-start | bytes 524288 | tf_op jit(solution)/shard_map/all_to_all | solution.py:115
  114.0 9.1 %all-to-all-done = f32[16,1,4096]{2,1,0:T(1,128)S(1)} async-done(((f32[16,1,4096]{2,1,0:T(1,128)}), f32[16,1,4096]{2,1,0:T(1,128)S(1)}, u32[]{:S(2)}, u32[]{:S(2)}) %all-to-all-start) | async-done | bytes 262176 | tf_op jit(solution)/shard_map/all_to_all | solution.py:115
  123.6 1.3 reduce.35
  124.8 1.0 reshape.636
  125.9 1.6 gather_fusion
  128.6 10.7 %all_to_all.10 = bf16[16,2,2048]{2,1,0:T(2,128)(2,1)S(1)} all-to-all(bf16[16,2,2048]{2,1,0:T(2,128)(2,1)S(1)} %reshape.637), channel_id=1, replica_groups=mesh['patch'=16,'chan'=2] {'patch'}, dimensions={0} | all-to-all | bytes 262144 | tf_op jit(solution)/shard_map/all_to_all | solution.py:129
  139.9 5.6 %all_gather.18 = bf16[128,1024]{1,0:T(8,128)(2,1)S(1)} all-gather(bf16[64,1024]{1,0:T(8,128)(2,1)S(1)} %reshape.572), channel_id=1, replica_groups=mesh['patch'=16,'chan'=2] {'chan'}, dimensions={0}, use_global_device_ids=true | all-gather | bytes 393216 | tf_op jit(solution)/shard_map/all_gather | solution.py:134
  146.4 1.0 pad.104
  147.5 1.2 convolution_bitcast_fusion.6
  151.2 1.7 pad_add_fusion
  152.9 2.5 reshape.575
  156.2 1.1 slice_bitcast_fusion.3
  158.3 2.4 slice.614
  161.7 1.0 fusion.19
  162.7 1.0 fusion.18
  163.6 1.0 fusion.17
  164.6 1.0 fusion.16
  165.5 1.0 fusion.15
  166.5 1.0 fusion.14
  167.4 1.0 fusion.13
  168.4 1.0 fusion.12
  169.4 27.6 %all-gather.9.cloned.1.call-done = f32[64,256,32]{1,2,0:T(8,128)} async-done(((f32[4,256,32]{1,2,0:T(8,128)}), f32[64,256,32]{1,2,0:T(8,128)}) %all-gather.9.cloned.1.call-update) | async-done | bytes 2097168 | tf_op jit(solution)/shard_map/all_gather | solution.py:163
  197.0 3.9 %rev.11 = f32[16,4,256,32]{2,3,1,0:T(8,128)} reverse(f32[16,4,256,32]{2,3,1,0:T(8,128)} %bitcast.319), dimensions={3} | reverse | bytes 4194304 | tf_op jit(solution)/shard_map/rev | solution.py:171
  200.8 3.6 %fusion.6 = f32[4,256,32]{1,0,2:T(4,128)S(1)} fusion(f32[16,4,256,32]{2,3,1,0:T(8,128)} %bitcast.320, s32[16,4]{0,1:T(4,128)S(1)} %add_select_fusion, pred[16,4]{0,1:T(4,128)(4,1)S(1)} %get-tuple-element.175, pred[16,4]{0,1:T(4,128)(4,1)S(1)} %get-tuple-element.182), kind=kOutput, calls=%fused_computation.43 | convolution fusion | flops 25166592 | bytes 2228608 | tf_op jit(solution)/shard_map/rst,rsep->tep/dot_general | solution.py:169
  204.5 2.0 fusion.30
  206.6 1.4 fusion.134
  208.0 1.4 fusion.133
  209.3 1.0 fusion.132
  210.3 1.8 scatter-add.16
  212.1 1.0 fusion.131
  213.1 1.8 scatter-add.19
  214.9 2.0 fusion.168
  220.6 1.0 copy-done.4
  223.2 38.6 %psum.28 = f32[]{:T(128)} all-reduce(f32[]{:T(128)} %fusion.59), channel_id=1, replica_groups=mesh['patch'=16,'chan'=2] {'patch','chan'}, use_global_device_ids=true, to_apply=%region_2.3 | all-reduce | flops 1 | bytes 8 | tf_op jit(solution)/shard_map/psum | solution.py:133
  262.4 32.4 %psum.31 = f32[256]{0:T(256)} all-reduce(f32[256]{0:T(256)S(1)} %get-tuple-element.150), channel_id=1, replica_groups=mesh['patch'=16,'chan'=2] {'patch'}, use_global_device_ids=true, to_apply=%region_7.8 | all-reduce | flops 256 | bytes 2048 | tf_op jit(solution)/shard_map/psum | solution.py:197
  294.8 25.3 %all-reduce.18.cloned.1.call-done = (f32[9,256,128]{2,1,0:T(8,128)}, f32[9,128,256]{2,1,0:T(8,128)}) async-done(((f32[9,256,128]{2,1,0:T(8,128)}, f32[9,128,256]{2,1,0:T(8,128)}), (f32[9,256,128]{2,1,0:T(8,128)}, f32[9,128,256]{2,1,0:T(8,128)})) %all-reduce.18.cloned.1.call-update) | async-done | bytes 2359312 | tf_op jit(solution)/shard_map/psum | solution.py:197
  320.2 2.5 copy.182
  322.6 1.0 copy.183
  (148 shorter events, 26.9 us)
Async XLA Ops:
  7.2 75.6 %all-gather.7.cloned.1.call-start = ((), (), s32[]{:S(2)}) async-start(), calls=%async_computation.3 | async-start | bytes 1114112 | tf_op jit(solution)/shard_map/all_gather | solution.py:100
  39.2 3.4 %copy-start.5 = (bf16[9,256,128]{2,1,0:T(8,128)(2,1)S(1)}, bf16[9,256,128]{2,1,0:T(8,128)(2,1)}, u32[]{:S(2)}) copy-start(bf16[9,256,128]{2,1,0:T(8,128)(2,1)} %param.34) | copy-start | bytes 1769476
  45.5 0.7 copy-start.12
  47.4 57.6 %reduce-scatter.4.cloned.1.call-start = ((), (), s32[]{:S(2)}) async-start(), calls=%async_computation.5 | async-start | bytes 786432
  84.7 2.5 copy-start.1
  90.2 1.0 copy-start.6
  90.3 1.2 copy-start.13
  106.1 6.9 %copy-start.10 = (bf16[1,1024]{1,0:T(2,128)(2,1)S(1)}, bf16[1,1024]{1,0:T(2,128)(2,1)}, u32[]{:S(2)}) copy-start(bf16[1,1024]{1,0:T(2,128)(2,1)} %param.41) | copy-start | bytes 6148
  106.1 7.0 %copy-start.7 = (bf16[1,64,1024]{2,1,0:T(8,128)(2,1)S(1)}, bf16[1,64,1024]{2,1,0:T(8,128)(2,1)}, u32[]{:S(2)}) copy-start(bf16[1,64,1024]{2,1,0:T(8,128)(2,1)} %param.40) | copy-start | bytes 393220
  107.4 15.7 %all-to-all-start = ((f32[16,1,4096]{2,1,0:T(1,128)}), f32[16,1,4096]{2,1,0:T(1,128)S(1)}, u32[]{:S(2)}, u32[]{:S(2)}) async-start(f32[16,1,4096]{2,1,0:T(1,128)} %reshape.635), calls=%async_computation | async-start | bytes 524288 | tf_op jit(solution)/shard_map/all_to_all | solution.py:115
  113.0 84.0 %all-gather.9.cloned.1.call-start = ((), (), s32[]{:S(2)}) async-start(), calls=%async_computation.4 | async-start | bytes 2228224 | tf_op jit(solution)/shard_map/all_gather | solution.py:163
  147.4 1.2 copy-start.2
  152.9 5.3 %copy-start.9 = (s32[16,4]{0,1:T(4,128)S(1)}, s32[16,4]{0,1:T(4,128)}, u32[]{:S(2)}) copy-start(s32[16,4]{0,1:T(4,128)} %param.38) | copy-start | bytes 772
  152.9 5.4 %copy-start.11 = (s32[16,4]{0,1:T(4,128)S(1)}, s32[16,4]{0,1:T(4,128)}, u32[]{:S(2)}) copy-start(s32[16,4]{0,1:T(4,128)} %param.37) | copy-start | bytes 772
  158.2 162.0 %all-reduce.18.cloned.1.call-start = ((), (), s32[]{:S(2)}) async-start(), calls=%async_computation.6 | async-start | bytes 4718592 | tf_op jit(solution)/shard_map/psum | solution.py:197
  200.8 3.6 %copy-start = (f32[16,4,256,32]{2,3,1,0:T(8,128)S(1)}, f32[16,4,256,32]{2,3,1,0:T(8,128)}, u32[]{:S(2)}) copy-start(f32[16,4,256,32]{2,3,1,0:T(8,128)} %rev.11) | copy-start | bytes 6291460
  220.6 1.0 copy-start.4
  221.6 0.9 copy-start.8
  320.2 2.5 copy-start.3
Sparse Core Ops, SparseCore 0:
  47.5 35.2 all-gather.6
  91.4 13.4 reduce-scatter.3
  158.3 38.5 all-gather.8
  221.7 98.3 all-reduce.17
where the time goes:
time: 332 us; the launch traced here: 331 us
  blocking collectives  118 us (36%)
  waiting for transfers between devices  110 us (33%)
  local copies, waits for them, and re-layouts  38.7 us (12%)
  matrix products  29.4 us (9%)
  between operations  16.4 us (5%)
  other arithmetic  12.4 us (4%)
  starting transfers between devices  5.79 us (2%)
    psum x1, blocking collectives, on_device(): lax.psum(partial_loss, ('patch', 'chan')) / (patch_count * cell_count * C)  38.6 us
    all_gather x1, waiting for transfers between devices, on_device(): lax.all_gather(edges_of(hidden_grid)[None], 'patch', axis=0, tiled=True)  35 us
    psum x1, blocking collectives, on_device(): lax.psum((one_local, two_local, bias_local), 'patch')  32.4 us
    all_gather x1, waiting for transfers between devices, on_device(): shard_rows = lax.all_gather(frames[None], 'patch', axis=0, tiled=True)  27.6 us
    psum x1, waiting for transfers between devices, on_device(): lax.psum((one_local, two_local, bias_local), 'patch')  25.3 us
    all_gather x1, blocking collectives, on_device(): lax.all_gather(edges_of(grid)[None], 'patch', axis=0, tiled=True)  23.5 us
    unnamed x5, waiting for transfers between devices  13.5 us
    all_to_all x1, blocking collectives, on_device(): lax.all_to_all(band_grad[:, inverse, :], 'patch', split_axis=1, concat_ax...  10.7 us
  transfers between devices with their start and end apart: 5, of which 5 were waited for; matrix products, arithmetic and copies ran while one was open for 4% of the time, Pallas kernels for 0%

commit v1 on v0

--- a/solution.py
+++ b/solution.py
@@ -160,7 +160,14 @@
             grad_frame[:, 1:-1, -1],
         ]
     )
-    shard_rows = lax.all_gather(frames[None], "patch", axis=0, tiled=True)
+    ring = [frames[None]]
+    for hop in range(15):
+        ring.append(lax.ppermute(ring[-1], "patch", [(dev, (dev + 1) % 16) for dev in range(16)]))
+    shard_rows = jnp.roll(
+        jnp.concatenate(ring[::-1], axis=0),
+        (lax.axis_index("patch") + 1) * ring[0].shape[0],
+        axis=0,
+    )
     matched = (neighbour == own_index)[:, :, None] & (
         (seam_code % 4)[:, :, None] == sides[None, None, :]
     )

time: 332 us -> 400 us (1.20)
  waiting for transfers between devices: 110 us -> 182 us
  local copies, waits for them, and re-layouts: 38.7 us -> 46.5 us
  matrix products: 29.4 us -> 22.5 us
  other arithmetic: 12.4 us -> 7.53 us
    ppermute x0 -> x15, waiting for transfers between devices: none -> 99.9 us  [on_device(): lax.ppermute(ring[-1], 'patch', [(dev, (dev + 1) % 16) for dev in range(1...]
    all_gather x1 -> x0, waiting for transfers between devices: 27.6 us -> none  [on_device(): shard_rows = lax.all_gather(frames[None], 'patch', axis=0, tiled=True)]
    concatenate x0 -> x1, local copies, waits for them, and re-layouts: none -> 15.6 us  [on_device(): jnp.roll(jnp.concatenate(ring[::-1], axis=0), (lax.axis_index('patch') +...]
    dot_general x9, matrix products: 8.61 us -> 2.67 us  [on_device(): lax.dot_general(grad_wide, h_taps[idx], (((1,), (1,)), ((), ())), preferr...]
    unnamed x47 -> x77, local copies, waits for them, and re-layouts: 10.4 us -> 12.2 us
    unnamed x5 -> x4, waiting for transfers between devices: 13.5 us -> 13.5 us
  transfers between devices with their start and end apart: 5 -> 19, of which waited for: 5 -> 19; matrix products, arithmetic and copies ran while one was open for 4% -> 2% of each run, Pallas kernels for 0% -> 0%
where the time goes in v1:
time: 400 us; the launch traced here: 398 us
  waiting for transfers between devices  182 us (46%)
  blocking collectives  116 us (29%)
  local copies, waits for them, and re-layouts  46.5 us (12%)
  matrix products  22.5 us (6%)
  between operations  16.7 us (4%)
  other arithmetic  7.53 us (2%)
  starting transfers between devices  5.84 us (1%)
    ppermute x15, waiting for transfers between devices, on_device(): lax.ppermute(ring[-1], 'patch', [(dev, (dev + 1) % 16) for dev in range(1...  99.9 us
    psum x1, blocking collectives, on_device(): lax.psum(partial_loss, ('patch', 'chan')) / (patch_count * cell_count * C)  37.3 us
    all_gather x1, waiting for transfers between devices, on_device(): lax.all_gather(edges_of(hidden_grid)[None], 'patch', axis=0, tiled=True)  35 us
    psum x1, blocking collectives, on_device(): lax.psum((one_local, two_local, bias_local), 'patch')  32 us
    psum x1, waiting for transfers between devices, on_device(): lax.psum((one_local, two_local, bias_local), 'patch')  24.9 us
    all_gather x1, blocking collectives, on_device(): lax.all_gather(edges_of(grid)[None], 'patch', axis=0, tiled=True)  23.5 us
    concatenate x1, local copies, waits for them, and re-layouts, on_device(): jnp.roll(jnp.concatenate(ring[::-1], axis=0), (lax.axis_index('patch') +...  15.6 us
    unnamed x4, waiting for transfers between devices  13.5 us
  transfers between devices with their start and end apart: 19, of which 19 were waited for; matrix products, arithmetic and copies ran while one was open for 2% of the time, Pallas kernels for 0%

profile of v1, /device:TPU:0, one launch (start us, length us, event | category | flops | bytes accessed | tf_op | source)
XLA Modules:
  0.0 397.6 jit_solution(9625856158023632429)
XLA Ops:
  7.2 7.4 %all-gather = bf16[1,128,1024]{2,1,0:T(8,128)(2,1)S(1)} all-gather(bf16[1,64,1024]{2,1,0:T(8,128)(2,1)} %param.33), channel_id=2, replica_groups=mesh['patch'=16,'chan'=2] {'chan'}, dimensions={1}, use_global_device_ids=true | all-gather | bytes 393216 | tf_op jit(solution)/shard_map/all_gather | solution.py:90
  14.8 0.9 dynamic-slice_reduce_fusion
  15.8 23.5 %all-gather.1 = bf16[64,128,32]{1,2,0:T(8,128)(2,1)S(1)} all-gather(bf16[4,128,32]{1,2,0:T(8,128)(2,1)S(1)} %pad_maximum_fusion.2), channel_id=3, replica_groups=mesh['patch'=16,'chan'=2] {'patch'}, dimensions={0}, use_global_device_ids=true | all-gather | bytes 557056 | tf_op jit(solution)/shard_map/all_gather | solution.py:92
  40.6 1.5 scatter.34
  45.5 1.2 reshape.563
  46.7 1.3 slice.596
  50.1 35.0 %all-gather.5.cloned.1.call-done = bf16[64,256,32]{1,2,0:T(8,128)(2,1)} async-done(((bf16[4,256,32]{1,2,0:T(8,128)(2,1)}), bf16[64,256,32]{1,2,0:T(8,128)(2,1)}) %all-gather.5.cloned.1.call-update) | async-done | bytes 1048592 | tf_op jit(solution)/shard_map/all_gather | solution.py:100
  85.0 2.0 convolution_bitcast_fusion.27
  87.3 1.4 scatter.40
  89.6 0.9 copy-done.2
  93.6 1.0 copy.110
  94.8 13.4 %reduce-scatter.4.cloned.1.call-done = f32[64,1024]{1,0:T(8,128)} async-done(((f32[128,1024]{1,0:T(8,128)}), f32[64,1024]{1,0:T(8,128)}) %reduce-scatter.4.cloned.1.call-update) | async-done | bytes 262160
  108.2 1.1 copy.111
  109.7 1.0 reshape.634
  110.7 5.6 %all-to-all-start = ((f32[16,1,4096]{2,1,0:T(1,128)}), f32[16,1,4096]{2,1,0:T(1,128)S(1)}, u32[]{:S(2)}, u32[]{:S(2)}) async-start(f32[16,1,4096]{2,1,0:T(1,128)} %reshape.634), calls=%async_computation | async-start | bytes 524288 | tf_op jit(solution)/shard_map/all_to_all | solution.py:115
  117.5 8.9 %all-to-all-done = f32[16,1,4096]{2,1,0:T(1,128)S(1)} async-done(((f32[16,1,4096]{2,1,0:T(1,128)}), f32[16,1,4096]{2,1,0:T(1,128)S(1)}, u32[]{:S(2)}, u32[]{:S(2)}) %all-to-all-start) | async-done | bytes 262176 | tf_op jit(solution)/shard_map/all_to_all | solution.py:115
  126.9 1.3 reduce.35
  130.1 10.7 %all_to_all.10 = bf16[16,2,2048]{2,1,0:T(2,128)(2,1)S(1)} all-to-all(bf16[16,2,2048]{2,1,0:T(2,128)(2,1)S(1)} %reshape.636), channel_id=1, replica_groups=mesh['patch'=16,'chan'=2] {'patch'}, dimensions={0} | all-to-all | bytes 262144 | tf_op jit(solution)/shard_map/all_to_all | solution.py:129
  141.4 5.6 %all_gather.15 = bf16[128,1024]{1,0:T(8,128)(2,1)S(1)} all-gather(bf16[64,1024]{1,0:T(8,128)(2,1)S(1)} %reshape.572), channel_id=1, replica_groups=mesh['patch'=16,'chan'=2] {'chan'}, dimensions={0}, use_global_device_ids=true | all-gather | bytes 393216 | tf_op jit(solution)/shard_map/all_gather | solution.py:134
  150.9 1.3 reshape.575
  153.0 1.1 slice_bitcast_fusion.4
  154.5 7.1 %collective-permute-done = f32[1,4,256,32]{2,0,1,3:T(1,128)S(1)} collective-permute-done((f32[1,4,256,32]{2,0,1,3:T(1,128)S(1)}, f32[1,4,256,32]{2,0,1,3:T(1,128)S(1)}, u32[]{:S(2)}, u32[]{:S(2)}) %collective-permute-start) | collective-permute-done | bytes 131104 | tf_op jit(solution)/shard_map/ppermute | solution.py:165
  161.5 7.2 %collective-permute-done.1 = f32[1,4,256,32]{2,0,1,3:T(1,128)} collective-permute-done((f32[1,4,256,32]{2,0,1,3:T(1,128)S(1)}, f32[1,4,256,32]{2,0,1,3:T(1,128)}, u32[]{:S(2)}, u32[]{:S(2)}) %collective-permute-start.1) | collective-permute-done | bytes 131104 | tf_op jit(solution)/shard_map/ppermute | solution.py:165
  168.7 7.3 %collective-permute-done.2 = f32[1,4,256,32]{2,0,1,3:T(1,128)S(1)} collective-permute-done((f32[1,4,256,32]{2,0,1,3:T(1,128)}, f32[1,4,256,32]{2,0,1,3:T(1,128)S(1)}, u32[]{:S(2)}, u32[]{:S(2)}) %collective-permute-start.2) | collective-permute-done | bytes 131104 | tf_op jit(solution)/shard_map/ppermute | solution.py:165
  176.0 7.1 %collective-permute-done.3 = f32[1,4,256,32]{2,0,1,3:T(1,128)S(1)} collective-permute-done((f32[1,4,256,32]{2,0,1,3:T(1,128)S(1)}, f32[1,4,256,32]{2,0,1,3:T(1,128)S(1)}, u32[]{:S(2)}, u32[]{:S(2)}) %collective-permute-start.3) | collective-permute-done | bytes 131104 | tf_op jit(solution)/shard_map/ppermute | solution.py:165
  183.7 6.5 %collective-permute-done.4 = f32[1,4,256,32]{2,0,1,3:T(1,128)S(1)} collective-permute-done((f32[1,4,256,32]{2,0,1,3:T(1,128)S(1)}, f32[1,4,256,32]{2,0,1,3:T(1,128)S(1)}, u32[]{:S(2)}, u32[]{:S(2)}) %collective-permute-start.4) | collective-permute-done | bytes 131104 | tf_op jit(solution)/shard_map/ppermute | solution.py:165
  190.3 1.5 slice.614
  192.4 4.9 %collective-permute-done.5 = f32[1,4,256,32]{2,0,1,3:T(1,128)S(1)} collective-permute-done((f32[1,4,256,32]{2,0,1,3:T(1,128)S(1)}, f32[1,4,256,32]{2,0,1,3:T(1,128)S(1)}, u32[]{:S(2)}, u32[]{:S(2)}) %collective-permute-start.5) | collective-permute-done | bytes 131104 | tf_op jit(solution)/shard_map/ppermute | solution.py:165
  197.6 6.8 %collective-permute-done.6 = f32[1,4,256,32]{2,0,1,3:T(1,128)S(1)} collective-permute-done((f32[1,4,256,32]{2,0,1,3:T(1,128)S(1)}, f32[1,4,256,32]{2,0,1,3:T(1,128)S(1)}, u32[]{:S(2)}, u32[]{:S(2)}) %collective-permute-start.6) | collective-permute-done | bytes 131104 | tf_op jit(solution)/shard_map/ppermute | solution.py:165
  204.7 6.8 %collective-permute-done.7 = f32[1,4,256,32]{2,0,1,3:T(1,128)S(1)} collective-permute-done((f32[1,4,256,32]{2,0,1,3:T(1,128)S(1)}, f32[1,4,256,32]{2,0,1,3:T(1,128)S(1)}, u32[]{:S(2)}, u32[]{:S(2)}) %collective-permute-start.7) | collective-permute-done | bytes 131104 | tf_op jit(solution)/shard_map/ppermute | solution.py:165
  211.8 6.8 %collective-permute-done.8 = f32[1,4,256,32]{2,0,1,3:T(1,128)S(1)} collective-permute-done((f32[1,4,256,32]{2,0,1,3:T(1,128)S(1)}, f32[1,4,256,32]{2,0,1,3:T(1,128)S(1)}, u32[]{:S(2)}, u32[]{:S(2)}) %collective-permute-start.8) | collective-permute-done | bytes 131104 | tf_op jit(solution)/shard_map/ppermute | solution.py:165
  218.9 6.8 %collective-permute-done.9 = f32[1,4,256,32]{2,0,1,3:T(1,128)S(1)} collective-permute-done((f32[1,4,256,32]{2,0,1,3:T(1,128)S(1)}, f32[1,4,256,32]{2,0,1,3:T(1,128)S(1)}, u32[]{:S(2)}, u32[]{:S(2)}) %collective-permute-start.9) | collective-permute-done | bytes 131104 | tf_op jit(solution)/shard_map/ppermute | solution.py:165
  226.0 6.8 %collective-permute-done.10 = f32[1,4,256,32]{2,0,1,3:T(1,128)S(1)} collective-permute-done((f32[1,4,256,32]{2,0,1,3:T(1,128)S(1)}, f32[1,4,256,32]{2,0,1,3:T(1,128)S(1)}, u32[]{:S(2)}, u32[]{:S(2)}) %collective-permute-start.10) | collective-permute-done | bytes 131104 | tf_op jit(solution)/shard_map/ppermute | solution.py:165
  233.1 6.8 %collective-permute-done.11 = f32[1,4,256,32]{2,0,1,3:T(1,128)S(1)} collective-permute-done((f32[1,4,256,32]{2,0,1,3:T(1,128)S(1)}, f32[1,4,256,32]{2,0,1,3:T(1,128)S(1)}, u32[]{:S(2)}, u32[]{:S(2)}) %collective-permute-start.11) | collective-permute-done | bytes 131104 | tf_op jit(solution)/shard_map/ppermute | solution.py:165
  240.2 6.8 %collective-permute-done.12 = f32[1,4,256,32]{2,0,1,3:T(1,128)S(1)} collective-permute-done((f32[1,4,256,32]{2,0,1,3:T(1,128)S(1)}, f32[1,4,256,32]{2,0,1,3:T(1,128)S(1)}, u32[]{:S(2)}, u32[]{:S(2)}) %collective-permute-start.12) | collective-permute-done | bytes 131104 | tf_op jit(solution)/shard_map/ppermute | solution.py:165
  247.3 6.8 %collective-permute-done.13 = f32[1,4,256,32]{2,0,1,3:T(1,128)S(1)} collective-permute-done((f32[1,4,256,32]{2,0,1,3:T(1,128)S(1)}, f32[1,4,256,32]{2,0,1,3:T(1,128)S(1)}, u32[]{:S(2)}, u32[]{:S(2)}) %collective-permute-start.13) | collective-permute-done | bytes 131104 | tf_op jit(solution)/shard_map/ppermute | solution.py:165
  254.7 1.0 copy-done.4
  255.7 5.5 %collective-permute-done.14 = f32[1,4,256,32]{2,0,1,3:T(1,128)} collective-permute-done((f32[1,4,256,32]{2,0,1,3:T(1,128)S(1)}, f32[1,4,256,32]{2,0,1,3:T(1,128)}, u32[]{:S(2)}, u32[]{:S(2)}) %collective-permute-start.14) | collective-permute-done | bytes 131104 | tf_op jit(solution)/shard_map/ppermute | solution.py:165
  261.3 15.6 %concatenate.34 = f32[32,4,256,32]{2,0,1,3:T(8,128)} concatenate(f32[1,4,256,32]{2,0,1,3:T(1,128)} %collective-permute-done.14, f32[1,4,256,32]{2,0,1,3:T(1,128)} %copy-done.19, f32[1,4,256,32]{2,0,1,3:T(1,128)} %copy-done.18, f32[1,4,256,32]{2,0,1,3:T(1,128)} %copy-done.17, f32[1,4,256,32]{2,0,1,3:T(1,128)} %copy-done.16, f32[1,4,256,32]{2,0,1,3:T(1,128)} %copy-done.15, ...), dimensions={0} | concatenate | bytes 8388608 | tf_op jit(solution)/shard_map/jit(_roll_dynamic)/concatenate | solution.py:166
  276.9 2.9 fusion.6
  279.7 2.9 fusion.9
  283.9 1.1 fusion.168
  289.0 1.0 copy-done.6
  291.6 37.3 %psum.28 = f32[]{:T(128)} all-reduce(f32[]{:T(128)} %fusion.56), channel_id=1, replica_groups=mesh['patch'=16,'chan'=2] {'patch','chan'}, use_global_device_ids=true, to_apply=%region_2.3 | all-reduce | flops 1 | bytes 8 | tf_op jit(solution)/shard_map/psum | solution.py:133
  329.6 32.0 %psum.31 = f32[256]{0:T(256)} all-reduce(f32[256]{0:T(256)S(1)} %get-tuple-element.150), channel_id=1, replica_groups=mesh['patch'=16,'chan'=2] {'patch'}, use_global_device_ids=true, to_apply=%region_7.8 | all-reduce | flops 256 | bytes 2048 | tf_op jit(solution)/shard_map/psum | solution.py:204
  361.6 24.9 %all-reduce.18.cloned.1.call-done = (f32[9,256,128]{2,1,0:T(8,128)}, f32[9,128,256]{2,1,0:T(8,128)}) async-done(((f32[9,256,128]{2,1,0:T(8,128)}, f32[9,128,256]{2,1,0:T(8,128)}), (f32[9,256,128]{2,1,0:T(8,128)}, f32[9,128,256]{2,1,0:T(8,128)})) %all-reduce.18.cloned.1.call-update) | async-done | bytes 2359312 | tf_op jit(solution)/shard_map/psum | solution.py:204
  386.5 2.5 copy.196
  388.9 1.0 copy.197
  (211 shorter events, 31.4 us)
Async XLA Ops:
  7.2 77.9 %all-gather.5.cloned.1.call-start = ((), (), s32[]{:S(2)}) async-start(), calls=%async_computation.3 | async-start | bytes 1114112 | tf_op jit(solution)/shard_map/all_gather | solution.py:100
  39.2 3.4 copy-start.7
  46.7 1.4 copy-start.26
  49.7 58.6 %reduce-scatter.4.cloned.1.call-start = ((), (), s32[]{:S(2)}) async-start(), calls=%async_computation.4 | async-start | bytes 786432
  89.5 1.1 copy-start.2
  93.5 1.1 copy-start.20
  93.6 1.2 copy-start.28
  109.4 6.9 %copy-start.24 = (bf16[1,1024]{1,0:T(2,128)(2,1)S(1)}, bf16[1,1024]{1,0:T(2,128)(2,1)}, u32[]{:S(2)}) copy-start(bf16[1,1024]{1,0:T(2,128)(2,1)} %param.41) | copy-start | bytes 6148
  109.5 7.0 %copy-start.21 = (bf16[1,64,1024]{2,1,0:T(8,128)(2,1)S(1)}, bf16[1,64,1024]{2,1,0:T(8,128)(2,1)}, u32[]{:S(2)}) copy-start(bf16[1,64,1024]{2,1,0:T(8,128)(2,1)} %param.40) | copy-start | bytes 393220
  110.7 15.7 %all-to-all-start = ((f32[16,1,4096]{2,1,0:T(1,128)}), f32[16,1,4096]{2,1,0:T(1,128)S(1)}, u32[]{:S(2)}, u32[]{:S(2)}) async-start(f32[16,1,4096]{2,1,0:T(1,128)} %reshape.634), calls=%async_computation | async-start | bytes 524288 | tf_op jit(solution)/shard_map/all_to_all | solution.py:115
  116.3 270.1 %all-reduce.18.cloned.1.call-start = ((), (), s32[]{:S(2)}) async-start(), calls=%async_computation.5 | async-start | bytes 4718592 | tf_op jit(solution)/shard_map/psum | solution.py:204
  129.0 0.9 copy-start
  141.2 6.2 %copy-start.3 = (bf16[9,128,256]{2,1,0:T(8,128)(2,1)S(1)}, bf16[9,128,256]{2,1,0:T(8,128)(2,1)}, u32[]{:S(2)}) copy-start(bf16[9,128,256]{2,1,0:T(8,128)(2,1)} %param.36) | copy-start | bytes 1769476
  150.9 32.2 %copy-start.23 = (s32[16,4]{0,1:T(4,128)S(1)}, s32[16,4]{0,1:T(4,128)}, u32[]{:S(2)}) copy-start(s32[16,4]{0,1:T(4,128)} %param.38) | copy-start | bytes 772
  150.9 32.2 %copy-start.25 = (s32[16,4]{0,1:T(4,128)S(1)}, s32[16,4]{0,1:T(4,128)}, u32[]{:S(2)}) copy-start(s32[16,4]{0,1:T(4,128)} %param.37) | copy-start | bytes 772
  154.4 7.1 %collective-permute-start = (f32[1,4,256,32]{2,0,1,3:T(1,128)S(1)}, f32[1,4,256,32]{2,0,1,3:T(1,128)S(1)}, u32[]{:S(2)}, u32[]{:S(2)}) collective-permute-start(f32[1,4,256,32]{2,0,1,3:T(1,128)S(1)} %broadcast_in_dim.32), channel_id=1, source_target_pairs={{0,2},{2,4},{4,6},{6,8},{8,10},{10,12},{12,14},{14,16},{16,18},{18... | collective-permute-start | bytes 393224 | tf_op jit(solution)/shard_map/ppermute | solution.py:165
  161.5 7.2 %collective-permute-start.1 = (f32[1,4,256,32]{2,0,1,3:T(1,128)S(1)}, f32[1,4,256,32]{2,0,1,3:T(1,128)}, u32[]{:S(2)}, u32[]{:S(2)}) collective-permute-start(f32[1,4,256,32]{2,0,1,3:T(1,128)S(1)} %collective-permute-done), channel_id=1, source_target_pairs={{0,2},{2,4},{4,6},{6,8},{8,10},{10,12},{12,14},{14,16},{16,18},{18... | collective-permute-start | bytes 393224 | tf_op jit(solution)/shard_map/ppermute | solution.py:165
  168.7 7.3 %collective-permute-start.2 = (f32[1,4,256,32]{2,0,1,3:T(1,128)}, f32[1,4,256,32]{2,0,1,3:T(1,128)S(1)}, u32[]{:S(2)}, u32[]{:S(2)}) collective-permute-start(f32[1,4,256,32]{2,0,1,3:T(1,128)} %collective-permute-done.1), channel_id=1, source_target_pairs={{0,2},{2,4},{4,6},{6,8},{8,10},{10,12},{12,14},{14,16},{16,18},{18... | collective-permute-start | bytes 393224 | tf_op jit(solution)/shard_map/ppermute | solution.py:165
  176.0 14.2 %copy-start.8 = (f32[1,4,256,32]{2,0,1,3:T(1,128)}, f32[1,4,256,32]{2,0,1,3:T(1,128)S(1)}, u32[]{:S(2)}) copy-start(f32[1,4,256,32]{2,0,1,3:T(1,128)S(1)} %collective-permute-done.2) | copy-start | bytes 393220
  176.0 7.1 %collective-permute-start.3 = (f32[1,4,256,32]{2,0,1,3:T(1,128)S(1)}, f32[1,4,256,32]{2,0,1,3:T(1,128)S(1)}, u32[]{:S(2)}, u32[]{:S(2)}) collective-permute-start(f32[1,4,256,32]{2,0,1,3:T(1,128)S(1)} %collective-permute-done.2), channel_id=1, source_target_pairs={{0,2},{2,4},{4,6},{6,8},{8,10},{10,12},{12,14},{14,16},{16,18},{18... | collective-permute-start | bytes 393224 | tf_op jit(solution)/shard_map/ppermute | solution.py:165
  183.1 7.1 %copy-start.9 = (f32[1,4,256,32]{2,0,1,3:T(1,128)}, f32[1,4,256,32]{2,0,1,3:T(1,128)S(1)}, u32[]{:S(2)}) copy-start(f32[1,4,256,32]{2,0,1,3:T(1,128)S(1)} %collective-permute-done.3) | copy-start | bytes 393220
  183.1 7.1 %collective-permute-start.4 = (f32[1,4,256,32]{2,0,1,3:T(1,128)S(1)}, f32[1,4,256,32]{2,0,1,3:T(1,128)S(1)}, u32[]{:S(2)}, u32[]{:S(2)}) collective-permute-start(f32[1,4,256,32]{2,0,1,3:T(1,128)S(1)} %collective-permute-done.3), channel_id=1, source_target_pairs={{0,2},{2,4},{4,6},{6,8},{8,10},{10,12},{12,14},{14,16},{16,18},{18... | collective-permute-start | bytes 393224 | tf_op jit(solution)/shard_map/ppermute | solution.py:165
  190.2 2.1 copy-start.10
  190.2 7.1 %collective-permute-start.5 = (f32[1,4,256,32]{2,0,1,3:T(1,128)S(1)}, f32[1,4,256,32]{2,0,1,3:T(1,128)S(1)}, u32[]{:S(2)}, u32[]{:S(2)}) collective-permute-start(f32[1,4,256,32]{2,0,1,3:T(1,128)S(1)} %collective-permute-done.4), channel_id=1, source_target_pairs={{0,2},{2,4},{4,6},{6,8},{8,10},{10,12},{12,14},{14,16},{16,18},{18... | collective-permute-start | bytes 393224 | tf_op jit(solution)/shard_map/ppermute | solution.py:165
  197.3 14.5 %copy-start.11 = (f32[1,4,256,32]{2,0,1,3:T(1,128)}, f32[1,4,256,32]{2,0,1,3:T(1,128)S(1)}, u32[]{:S(2)}) copy-start(f32[1,4,256,32]{2,0,1,3:T(1,128)S(1)} %collective-permute-done.5) | copy-start | bytes 393220
  197.3 7.1 %collective-permute-start.6 = (f32[1,4,256,32]{2,0,1,3:T(1,128)S(1)}, f32[1,4,256,32]{2,0,1,3:T(1,128)S(1)}, u32[]{:S(2)}, u32[]{:S(2)}) collective-permute-start(f32[1,4,256,32]{2,0,1,3:T(1,128)S(1)} %collective-permute-done.5), channel_id=1, source_target_pairs={{0,2},{2,4},{4,6},{6,8},{8,10},{10,12},{12,14},{14,16},{16,18},{18... | collective-permute-start | bytes 393224 | tf_op jit(solution)/shard_map/ppermute | solution.py:165
  204.4 7.4 %copy-start.12 = (f32[1,4,256,32]{2,0,1,3:T(1,128)}, f32[1,4,256,32]{2,0,1,3:T(1,128)S(1)}, u32[]{:S(2)}) copy-start(f32[1,4,256,32]{2,0,1,3:T(1,128)S(1)} %collective-permute-done.6) | copy-start | bytes 393220
  204.4 7.1 %collective-permute-start.7 = (f32[1,4,256,32]{2,0,1,3:T(1,128)S(1)}, f32[1,4,256,32]{2,0,1,3:T(1,128)S(1)}, u32[]{:S(2)}, u32[]{:S(2)}) collective-permute-start(f32[1,4,256,32]{2,0,1,3:T(1,128)S(1)} %collective-permute-done.6), channel_id=1, source_target_pairs={{0,2},{2,4},{4,6},{6,8},{8,10},{10,12},{12,14},{14,16},{16,18},{18... | collective-permute-start | bytes 393224 | tf_op jit(solution)/shard_map/ppermute | solution.py:165
  211.5 7.4 %copy-start.13 = (f32[1,4,256,32]{2,0,1,3:T(1,128)}, f32[1,4,256,32]{2,0,1,3:T(1,128)S(1)}, u32[]{:S(2)}) copy-start(f32[1,4,256,32]{2,0,1,3:T(1,128)S(1)} %collective-permute-done.7) | copy-start | bytes 393220
  211.5 7.1 %collective-permute-start.8 = (f32[1,4,256,32]{2,0,1,3:T(1,128)S(1)}, f32[1,4,256,32]{2,0,1,3:T(1,128)S(1)}, u32[]{:S(2)}, u32[]{:S(2)}) collective-permute-start(f32[1,4,256,32]{2,0,1,3:T(1,128)S(1)} %collective-permute-done.7), channel_id=1, source_target_pairs={{0,2},{2,4},{4,6},{6,8},{8,10},{10,12},{12,14},{14,16},{16,18},{18... | collective-permute-start | bytes 393224 | tf_op jit(solution)/shard_map/ppermute | solution.py:165
  218.6 7.4 %copy-start.14 = (f32[1,4,256,32]{2,0,1,3:T(1,128)}, f32[1,4,256,32]{2,0,1,3:T(1,128)S(1)}, u32[]{:S(2)}) copy-start(f32[1,4,256,32]{2,0,1,3:T(1,128)S(1)} %collective-permute-done.8) | copy-start | bytes 393220
  218.6 7.1 %collective-permute-start.9 = (f32[1,4,256,32]{2,0,1,3:T(1,128)S(1)}, f32[1,4,256,32]{2,0,1,3:T(1,128)S(1)}, u32[]{:S(2)}, u32[]{:S(2)}) collective-permute-start(f32[1,4,256,32]{2,0,1,3:T(1,128)S(1)} %collective-permute-done.8), channel_id=1, source_target_pairs={{0,2},{2,4},{4,6},{6,8},{8,10},{10,12},{12,14},{14,16},{16,18},{18... | collective-permute-start | bytes 393224 | tf_op jit(solution)/shard_map/ppermute | solution.py:165
  225.7 7.4 %copy-start.15 = (f32[1,4,256,32]{2,0,1,3:T(1,128)}, f32[1,4,256,32]{2,0,1,3:T(1,128)S(1)}, u32[]{:S(2)}) copy-start(f32[1,4,256,32]{2,0,1,3:T(1,128)S(1)} %collective-permute-done.9) | copy-start | bytes 393220
  225.7 7.1 %collective-permute-start.10 = (f32[1,4,256,32]{2,0,1,3:T(1,128)S(1)}, f32[1,4,256,32]{2,0,1,3:T(1,128)S(1)}, u32[]{:S(2)}, u32[]{:S(2)}) collective-permute-start(f32[1,4,256,32]{2,0,1,3:T(1,128)S(1)} %collective-permute-done.9), channel_id=1, source_target_pairs={{0,2},{2,4},{4,6},{6,8},{8,10},{10,12},{12,14},{14,16},{16,18},{18... | collective-permute-start | bytes 393224 | tf_op jit(solution)/shard_map/ppermute | solution.py:165
  232.8 7.4 %copy-start.16 = (f32[1,4,256,32]{2,0,1,3:T(1,128)}, f32[1,4,256,32]{2,0,1,3:T(1,128)S(1)}, u32[]{:S(2)}) copy-start(f32[1,4,256,32]{2,0,1,3:T(1,128)S(1)} %collective-permute-done.10) | copy-start | bytes 393220
  232.8 7.1 %collective-permute-start.11 = (f32[1,4,256,32]{2,0,1,3:T(1,128)S(1)}, f32[1,4,256,32]{2,0,1,3:T(1,128)S(1)}, u32[]{:S(2)}, u32[]{:S(2)}) collective-permute-start(f32[1,4,256,32]{2,0,1,3:T(1,128)S(1)} %collective-permute-done.10), channel_id=1, source_target_pairs={{0,2},{2,4},{4,6},{6,8},{8,10},{10,12},{12,14},{14,16},{16,18},{18... | collective-permute-start | bytes 393224 | tf_op jit(solution)/shard_map/ppermute | solution.py:165
  239.9 7.4 %copy-start.17 = (f32[1,4,256,32]{2,0,1,3:T(1,128)}, f32[1,4,256,32]{2,0,1,3:T(1,128)S(1)}, u32[]{:S(2)}) copy-start(f32[1,4,256,32]{2,0,1,3:T(1,128)S(1)} %collective-permute-done.11) | copy-start | bytes 393220
  239.9 7.1 %collective-permute-start.12 = (f32[1,4,256,32]{2,0,1,3:T(1,128)S(1)}, f32[1,4,256,32]{2,0,1,3:T(1,128)S(1)}, u32[]{:S(2)}, u32[]{:S(2)}) collective-permute-start(f32[1,4,256,32]{2,0,1,3:T(1,128)S(1)} %collective-permute-done.11), channel_id=1, source_target_pairs={{0,2},{2,4},{4,6},{6,8},{8,10},{10,12},{12,14},{14,16},{16,18},{18... | collective-permute-start | bytes 393224 | tf_op jit(solution)/shard_map/ppermute | solution.py:165
  247.0 7.4 %copy-start.18 = (f32[1,4,256,32]{2,0,1,3:T(1,128)}, f32[1,4,256,32]{2,0,1,3:T(1,128)S(1)}, u32[]{:S(2)}) copy-start(f32[1,4,256,32]{2,0,1,3:T(1,128)S(1)} %collective-permute-done.12) | copy-start | bytes 393220
  247.0 7.1 %collective-permute-start.13 = (f32[1,4,256,32]{2,0,1,3:T(1,128)S(1)}, f32[1,4,256,32]{2,0,1,3:T(1,128)S(1)}, u32[]{:S(2)}, u32[]{:S(2)}) collective-permute-start(f32[1,4,256,32]{2,0,1,3:T(1,128)S(1)} %collective-permute-done.12), channel_id=1, source_target_pairs={{0,2},{2,4},{4,6},{6,8},{8,10},{10,12},{12,14},{14,16},{16,18},{18... | collective-permute-start | bytes 393224 | tf_op jit(solution)/shard_map/ppermute | solution.py:165
  254.1 0.7 copy-start.19
  254.1 7.2 %collective-permute-start.14 = (f32[1,4,256,32]{2,0,1,3:T(1,128)S(1)}, f32[1,4,256,32]{2,0,1,3:T(1,128)}, u32[]{:S(2)}, u32[]{:S(2)}) collective-permute-start(f32[1,4,256,32]{2,0,1,3:T(1,128)S(1)} %collective-permute-done.13), channel_id=1, source_target_pairs={{0,2},{2,4},{4,6},{6,8},{8,10},{10,12},{12,14},{14,16},{16,18},{18... | collective-permute-start | bytes 393224 | tf_op jit(solution)/shard_map/ppermute | solution.py:165
  254.7 1.0 copy-start.4
  255.7 21.2 %copy-start.27 = (pred[16,4]{0,1:T(4,128)(4,1)S(1)}, pred[16,4]{0,1:T(4,128)(4,1)}, u32[]{:S(2)}) copy-start(pred[16,4]{0,1:T(4,128)(4,1)} %get-tuple-element.172) | copy-start | bytes 196
  288.9 1.0 copy-start.6
  289.0 1.4 copy-start.1
  290.0 0.9 copy-start.22
  386.5 2.5 copy-start.5
Sparse Core Ops, SparseCore 0:
  49.8 35.2 all-gather.4
  94.7 13.4 reduce-scatter.3
  290.1 96.2 all-reduce.17
